TPU v7x, 512 devices: a whole 4x4x16 slice. The times are simulated.
512 devices in a mesh: prompt: 32 (over y, z_hi, core), sample: 16 (over z_lo, x).
Axes of the slice: x: 4, y: 4, z: 16 (z_hi: 4, z_lo: 4; z = z_hi * 4 + z_lo), core: 2. Of those that a mesh axis runs over, the one named last changes fastest.
Arguments:
- queries: bfloat16 [32, 8192, 1792], P('prompt', 'sample'), may hold values from -60 to 60
- prompt_keys: bfloat16 [32, 1024, 256], P('prompt', 'sample'), may hold values from -4 to 4
- prompt_value_rows: bfloat16 [32, 1024, 256], P('prompt', 'sample'), may hold values from -4 to 4
- reply_keys: bfloat16 [32, 8192, 256], P('prompt', 'sample'), may hold values from -4 to 4
- response_values: bfloat16 [32, 8192, 256], P('prompt', 'sample'), may hold values from -4 to 4
- lengths: int32 [32, 16], P('prompt'), may hold values from 1 to 4, as said below
- hand_counts: int32 [32, 16, 2], P('prompt'), may hold values from 0 to 2, as said below
Outputs:
- attended: bfloat16 [32, 8192, 1792], P('prompt', 'sample')
Inputs may be any that keep to these rules, and one draw needn't show every extreme that they name: lengths[p, s] counts the live tiles of response s; some response of every prompt has 4 tiles. hand_counts[p, s, k] is the number of tiles that device s hands to its section-k partner; of two partners at most one hands tiles, and every load stays between 1 and 4.
All inputs are finite; a program needn't handle non-finite values.
Results may differ from a plain program's by a relative error of at most 0.0038.
Values may be sent and summed in bfloat16 or wider, within the bound.
A program may use at most 64 MiB of HBM per device.

v0:
```python
import functools
import math

import jax
import jax.numpy as jnp
from jax import lax
from jax.experimental import pallas as pl
from jax.experimental.pallas import tpu as pltpu
from jax.sharding import PartitionSpec as P

KEY_VALUE_HEADS = 2
QUERY_PER_KEY = 7
HEADS = KEY_VALUE_HEADS * QUERY_PER_KEY
HEAD_WIDTH = 128
TILE_TOKENS = 128
MOST_TILES = 4
ALONG_X = 4
ALONG_Z = 4
LAG_SECOND = 2
LAG_OUT = 4

LOG_SCALE = math.log2(math.e) / math.sqrt(HEAD_WIDTH)


def dot_nt(a, b):
    return lax.dot_general(a, b, (((1,), (1,)), ((), ())), preferred_element_type=jnp.float32)


def softmax_parts(scores):
    top = jnp.max(scores, axis=-1, keepdims=True)
    weights = jnp.exp2((scores - top) * LOG_SCALE)
    total = jnp.sum(weights, axis=-1, keepdims=True)
    return top, weights.astype(jnp.bfloat16), total


def weigh(weights, values):
    return jnp.dot(weights, values, preferred_element_type=jnp.float32)


def reply_part(query, keys, values, half):
    rows = 2 * TILE_TOKENS
    seen = (half + 1) * rows
    scores = dot_nt(query, keys[:seen])
    row = lax.broadcasted_iota(jnp.int32, (rows, rows), 0)
    col = lax.broadcasted_iota(jnp.int32, (rows, rows), 1)
    last = jnp.where(col <= row, scores[:, half * rows :], -1e30)
    if half:
        last = jnp.concatenate([scores[:, : half * rows], last], axis=1)
    top, weights, total = softmax_parts(last)
    return top, total, weigh(weights, values[:seen])


def combine(p_top, p_total, p_mix, r_top, r_total, r_mix):
    top = jnp.maximum(p_top, r_top)
    a = jnp.exp2((p_top - top) * LOG_SCALE)
    b = jnp.exp2((r_top - top) * LOG_SCALE)
    inverse = 1.0 / (a * p_total + b * r_total)
    return (p_mix * (a * inverse) + r_mix * (b * inverse)).astype(jnp.bfloat16)


def kernel(
    q_hbm, pk_hbm, pv_hbm, rk_hbm, rv_hbm, len_ref, hand_ref, out_hbm,
    q_buf, kv, rkv, own, send1, recv1, send2, recv2, out_buf,
    in_sem, own_sem, z_send, z_recv, x_send, x_recv, d_send, d_recv,
    s1_sem, r1_sem, s2_sem, r2_sem, out_sem,
):
    me = lax.axis_index("sample")
    z = me // ALONG_X
    x = me % ALONG_X

    def at(zz, xx):
        return {"sample": zz * ALONG_X + xx}

    z_peers = [at((z + d) % ALONG_Z, x) for d in (1, 2, 3)]
    right = at(z, (x + 1) % ALONG_X)
    left = at(z, (x + 3) % ALONG_X)
    first_partner = z_peers[1]
    second_partner = at(z + 1 - 2 * (z % 2), x)
    MESH = pl.DeviceIdType.MESH

    barrier = pltpu.get_barrier_semaphore()
    for peer in z_peers + [right, left]:
        pl.semaphore_signal(barrier, inc=1, device_id=peer, device_id_type=MESH)

    width = HEAD_WIDTH
    own_rows = pl.ds(pl.multiple_of(x * 256 + z * 64, 64), 64)
    prompt_side = (pk_hbm, pv_hbm)
    reply_side = (rk_hbm, rv_hbm)
    own_copies = [
        pltpu.make_async_copy(
            prompt_side[kind].at[:, g * width : (g + 1) * width],
            kv.at[g, kind, own_rows, :],
            own_sem.at[g, kind],
        )
        for g in range(2)
        for kind in range(2)
    ]
    in_copies = [pltpu.make_async_copy(q_hbm, q_buf, in_sem.at[0])] + [
        pltpu.make_async_copy(
            reply_side[kind].at[:, g * width : (g + 1) * width],
            rkv.at[g, kind],
            in_sem.at[1 + 2 * g + kind],
        )
        for g in range(2)
        for kind in range(2)
    ]
    for copy in own_copies + in_copies:
        copy.start()

    def partner_of(mask_z):
        return ((z + 2) % 4 if mask_z == 2 else z + 1 - 2 * (z % 2)) * ALONG_X + x

    give1 = hand_ref[0, 0, me]
    get1 = hand_ref[0, 0, partner_of(2)]
    give2 = hand_ref[0, 1, me]
    get2 = hand_ref[0, 1, partner_of(1)]
    keep1 = len_ref[0, me] - give1
    keep2 = keep1 + get1 - give2
    load2 = keep2 + get2

    def z_copy(g, kind, d):
        return pltpu.make_async_remote_copy(
            prompt_side[kind].at[:, g * width : (g + 1) * width],
            kv.at[g, kind, own_rows, :],
            z_send.at[g, kind, d],
            z_recv.at[g, kind, d],
            device_id=z_peers[d],
            device_id_type=MESH,
        )

    def column(g, xx):
        return kv.at[g, :, pl.ds(pl.multiple_of(xx * 256, 256), 256), :]

    def half_column(g, kind, xx):
        return kv.at[g, kind, pl.ds(pl.multiple_of(xx * 256, 256), 256), :]

    def x_copy(g, way):
        return pltpu.make_async_remote_copy(
            column(g, x), column(g, x), x_send.at[g, way], x_recv.at[g, way],
            device_id=(right, left)[way], device_id_type=MESH,
        )

    def d_copy(g, way):
        source = ((x + 3) % ALONG_X, (x + 1) % ALONG_X)[way]
        return pltpu.make_async_remote_copy(
            half_column(g, way, source), half_column(g, way, source),
            d_send.at[g, way], d_recv.at[g, way],
            device_id=(right, left)[way], device_id_type=MESH,
        )

    pl.semaphore_wait(barrier, 5)
    for g in range(2):
        for d in (1, 0, 2):
            for kind in range(2):
                z_copy(g, kind, d).start()
    for copy in own_copies:
        copy.wait()
    for g in range(2):
        for d in range(3):
            for kind in range(2):
                z_copy(g, kind, d).wait_recv()
        for way in range(2):
            x_copy(g, way).start()
    for copy in in_copies:
        copy.wait()

    def forward_diagonal(g):
        for way in range(2):
            x_copy(g, way).wait_recv()
            d_copy(g, way).start()

    def gathered(g):
        for way in range(2):
            d_copy(g, way).wait_recv()

    forward_diagonal(0)

    def s1_copy(c):
        return pltpu.make_async_remote_copy(
            send1.at[c], recv1.at[c], s1_sem.at[c], r1_sem.at[c],
            device_id=first_partner, device_id_type=MESH,
        )

    def s2_copy(c):
        return pltpu.make_async_remote_copy(
            send2.at[c], recv2.at[c], s2_sem.at[c], r2_sem.at[c],
            device_id=second_partner, device_id_type=MESH,
        )

    def out_copy(c):
        return pltpu.make_async_copy(
            out_buf.at[c],
            out_hbm.at[:, :, pl.ds(pl.multiple_of(c * width, width), width)],
            out_sem.at[c],
        )

    def top_two(keep, one, two, three):
        first = jnp.where(keep == 1, one, jnp.where(keep == 2, two, three))
        return first, jnp.where(keep == 1, two, three)

    def placed(keep, one, two, three, a, b):
        return (
            jnp.where(keep == 1, a, one),
            jnp.where(keep == 1, b, jnp.where(keep == 2, a, two)),
            jnp.where(keep == 2, b, jnp.where(keep == 3, a, three)),
        )

    def attend(c):
        g = c // QUERY_PER_KEY
        cols = pl.ds(pl.multiple_of(c * width, width), width)
        rows = 2 * TILE_TOKENS
        reply = [
            reply_part(q_buf[h * rows : (h + 1) * rows, cols], rkv.at[g, 0], rkv.at[g, 1], h)
            for h in range(2)
        ]

        @pl.when(c == 0)
        def _():
            gathered(0)

        @pl.when(c == QUERY_PER_KEY)
        def _():
            gathered(1)

        tiles = []
        for h in range(2):
            scores = dot_nt(q_buf[h * rows : (h + 1) * rows, cols], kv[g, 0])
            top, weights, total = softmax_parts(scores)
            mix = weigh(weights, kv[g, 1])
            r_top, r_total, r_mix = reply[h]
            result = combine(top, total, mix, r_top, r_total, r_mix)
            tiles += [result[:TILE_TOKENS], result[TILE_TOKENS:]]
        for t in range(MOST_TILES):
            own[c, t] = tiles[t]
        first, second = top_two(keep1, tiles[1], tiles[2], tiles[3])
        send1[c, 0] = first
        send1[c, 1] = second

    def step(c, _):
        @pl.when(c < HEADS)
        def _():
            attend(c)
            s1_copy(c).start()

        @pl.when(c == 0)
        def _():
            forward_diagonal(1)

        @pl.when((c >= LAG_SECOND) & (c < HEADS + LAG_SECOND))
        def _():
            d = c - LAG_SECOND
            s1_copy(d).wait_recv()
            slots = placed(keep1, own[d, 1], own[d, 2], own[d, 3], recv1[d, 0], recv1[d, 1])
            first, second = top_two(keep2, *slots)
            send2[d, 0] = first
            send2[d, 1] = second
            s2_copy(d).start()
            for t in range(3):
                own[d, t + 1] = slots[t]

        @pl.when(c >= LAG_OUT)
        def _():
            e = c - LAG_OUT
            s2_copy(e).wait_recv()
            slots = placed(keep2, own[e, 1], own[e, 2], own[e, 3], recv2[e, 0], recv2[e, 1])
            out_buf[e, 0] = own[e, 0]
            for t in range(3):
                out_buf[e, t + 1] = jnp.where(t + 1 < load2, slots[t], jnp.zeros_like(slots[t]))
            out_copy(e).start()

        return 0

    lax.fori_loop(0, HEADS + LAG_OUT, step, 0)

    for g in range(2):
        for d in range(3):
            for kind in range(2):
                z_copy(g, kind, d).wait_send()
        for way in range(2):
            x_copy(g, way).wait_send()
            d_copy(g, way).wait_send()

    def finish(c, _):
        s1_copy(c).wait_send()
        s2_copy(c).wait_send()
        out_copy(c).wait()
        return 0

    lax.fori_loop(0, HEADS, finish, 0)


def per_device(
    queries, prompt_keys, prompt_value_rows, reply_keys, response_values, lengths, hand_counts
):
    half = jnp.bfloat16
    pair = (HEADS, 2, TILE_TOKENS, HEAD_WIDTH)
    four = (HEADS, MOST_TILES, TILE_TOKENS, HEAD_WIDTH)
    dma = pltpu.SemaphoreType.DMA
    anywhere = pl.BlockSpec(memory_space=pl.ANY)
    scalars = pl.BlockSpec(memory_space=pltpu.SMEM)
    out = pl.pallas_call(
        kernel,
        out_shape=jax.ShapeDtypeStruct((MOST_TILES, TILE_TOKENS, HEADS * HEAD_WIDTH), half),
        in_specs=[anywhere] * 5 + [scalars] * 2,
        out_specs=anywhere,
        scratch_shapes=[
            pltpu.VMEM((MOST_TILES * TILE_TOKENS, HEADS * HEAD_WIDTH), half),
            pltpu.VMEM((2, 2, 1024, HEAD_WIDTH), half),
            pltpu.VMEM((2, 2, MOST_TILES * TILE_TOKENS, HEAD_WIDTH), half),
            pltpu.VMEM(four, half),
            pltpu.VMEM(pair, half),
            pltpu.VMEM(pair, half),
            pltpu.VMEM(pair, half),
            pltpu.VMEM(pair, half),
            pltpu.VMEM(four, half),
            dma((5,)),
            dma((2, 2)),
            dma((2, 2, 3)),
            dma((2, 2, 3)),
            dma((2, 2)),
            dma((2, 2)),
            dma((2, 2)),
            dma((2, 2)),
            dma((HEADS,)),
            dma((HEADS,)),
            dma((HEADS,)),
            dma((HEADS,)),
            dma((HEADS,)),
        ],
        compiler_params=pltpu.CompilerParams(
            collective_id=0, has_side_effects=True, vmem_limit_bytes=56 << 20
        ),
    )(
        queries[0], prompt_keys[0], prompt_value_rows[0], reply_keys[0], response_values[0],
        lengths, jnp.swapaxes(hand_counts, 1, 2),
    )
    return out.reshape(1, MOST_TILES * TILE_TOKENS, -1)


def solution(mesh):
    placed = (
        P("prompt", "sample", None),
        P("prompt", "sample", None),
        P("prompt", "sample", None),
        P("prompt", "sample", None),
        P("prompt", "sample", None),
        P("prompt", None),
        P("prompt", None, None),
    )
    return jax.shard_map(
        per_device,
        mesh=mesh,
        in_specs=placed,
        out_specs=P("prompt", "sample", None),
        check_vma=False,
    )
```

profile of v0, /device:TPU:136, one launch (start us, length us, event | category | flops | bytes accessed | tf_op | source)
XLA Modules:
  0.0 72.3 jit_solution(3897917700168551574)
XLA Ops:
  0.0 69.5 %shard_map.73 = bf16[4,128,1792]{2,1,0:T(8,128)(2,1)} custom-call(bf16[512,1792]{1,0:T(8,128)(2,1)} %bitcast.8, bf16[64,256]{1,0:T(8,128)(2,1)} %bitcast.11, bf16[64,256]{1,0:T(8,128)(2,1)} %bitcast.12, bf16[512,256]{1,0:T(8,128)(2,1)} %bitcast.9, bf16[512,256]{1,0:T(8,128)(2,1)} %bitcast.10, s32[1,16]{1,0:T(1,128)} %len_ref.1, s32[1,2,16]{2,1,0:T(2,128)} %bitcast.13), custom_call_target="tpu_custom_call" | custom-call | tf_op jit(solution)/shard_map/pallas_call | solution.py:301
  69.5 2.8 %copy.9 = bf16[1,512,1792]{2,1,0:T(8,128)(2,1)} copy(bf16[1,512,1792]{2,1,0:T(8,128)(2,1)} %bitcast.7) | data formatting | bytes 3670016
where the time goes:
time: 72.5 us; the launch traced here: 72.3 us
  Pallas kernels  69.5 us (96%)
  local copies, waits for them, and re-layouts  2.85 us (4%)
    pallas_call x1, Pallas kernels, per_device(): pl.pallas_call(kernel, out_shape=jax.ShapeDtypeStruct((MOST_TILES, TILE_T...  69.5 us
    unnamed x1, local copies, waits for them, and re-layouts  2.85 us

commit v1 on v0

--- a/solution.py
+++ b/solution.py
@@ -16,8 +16,11 @@
 MOST_TILES = 4
 ALONG_X = 4
 ALONG_Z = 4
-LAG_SECOND = 2
-LAG_OUT = 4
+LAG_SECOND = 3
+LAG_OUT = 6
+PARTS = 1
+EARLY_FROM = 4
+EARLY = 1
 
 LOG_SCALE = math.log2(math.e) / math.sqrt(HEAD_WIDTH)
 
@@ -50,6 +53,15 @@
     return top, total, weigh(weights, values[:seen])
 
 
+def combine_level(p_top, p_total, p_mix, r_level, r_mix):
+    p_level = p_top * LOG_SCALE
+    top = jnp.maximum(p_level, r_level)
+    a = jnp.exp2(p_level - top)
+    b = jnp.exp2(r_level - top)
+    inverse = 1.0 / (a * p_total + b)
+    return (p_mix * (a * inverse) + r_mix.astype(jnp.float32) * (b * inverse)).astype(jnp.bfloat16)
+
+
 def combine(p_top, p_total, p_mix, r_top, r_total, r_mix):
     top = jnp.maximum(p_top, r_top)
     a = jnp.exp2((p_top - top) * LOG_SCALE)
@@ -61,8 +73,9 @@
 def kernel(
     q_hbm, pk_hbm, pv_hbm, rk_hbm, rv_hbm, len_ref, hand_ref, out_hbm,
     q_buf, kv, rkv, own, send1, recv1, send2, recv2, out_buf,
-    in_sem, own_sem, z_send, z_recv, x_send, x_recv, d_send, d_recv,
-    s1_sem, r1_sem, s2_sem, r2_sem, out_sem,
+    e_send, e_recv, l_send, l_recv,
+    in_sem, own_sem, z_send, z_recv, x_send, x_recv,
+    s1_sem, r1_sem, s2_sem, r2_sem, out_sem, es_sem, er_sem,
 ):
     me = lax.axis_index("sample")
     z = me // ALONG_X
@@ -71,15 +84,17 @@
     def at(zz, xx):
         return {"sample": zz * ALONG_X + xx}
 
-    z_peers = [at((z + d) % ALONG_Z, x) for d in (1, 2, 3)]
+    depths = [z, z + 1 - 2 * (z % 2), (z + 2) % ALONG_Z, ALONG_Z - 1 - z]
+    z_peers = [at(depth, x) for depth in depths[1:]]
+    across = at(z, (x + 2) % ALONG_X)
     right = at(z, (x + 1) % ALONG_X)
     left = at(z, (x + 3) % ALONG_X)
     first_partner = z_peers[1]
-    second_partner = at(z + 1 - 2 * (z % 2), x)
+    second_partner = z_peers[0]
     MESH = pl.DeviceIdType.MESH
 
     barrier = pltpu.get_barrier_semaphore()
-    for peer in z_peers + [right, left]:
+    for peer in z_peers + [right, left, across]:
         pl.semaphore_signal(barrier, inc=1, device_id=peer, device_id_type=MESH)
 
     width = HEAD_WIDTH
@@ -107,83 +122,115 @@
     for copy in own_copies + in_copies:
         copy.start()
 
-    def partner_of(mask_z):
-        return ((z + 2) % 4 if mask_z == 2 else z + 1 - 2 * (z % 2)) * ALONG_X + x
-
+    first_index = depths[2] * ALONG_X + x
+    second_index = depths[1] * ALONG_X + x
     give1 = hand_ref[0, 0, me]
-    get1 = hand_ref[0, 0, partner_of(2)]
+    get1 = hand_ref[0, 0, first_index]
     give2 = hand_ref[0, 1, me]
-    get2 = hand_ref[0, 1, partner_of(1)]
+    get2 = hand_ref[0, 1, second_index]
     keep1 = len_ref[0, me] - give1
     keep2 = keep1 + get1 - give2
     load2 = keep2 + get2
 
-    def z_copy(g, kind, d):
+    def block_rows(zz, xx):
+        return pl.ds(pl.multiple_of(xx * 256 + zz * 64, 64), 64)
+
+    def z_copy(g, i):
+        own_block = kv.at[g, :, own_rows, :]
         return pltpu.make_async_remote_copy(
-            prompt_side[kind].at[:, g * width : (g + 1) * width],
-            kv.at[g, kind, own_rows, :],
-            z_send.at[g, kind, d],
-            z_recv.at[g, kind, d],
-            device_id=z_peers[d],
-            device_id_type=MESH,
-        )
-
-    def column(g, xx):
-        return kv.at[g, :, pl.ds(pl.multiple_of(xx * 256, 256), 256), :]
-
-    def half_column(g, kind, xx):
-        return kv.at[g, kind, pl.ds(pl.multiple_of(xx * 256, 256), 256), :]
-
-    def x_copy(g, way):
+            own_block, own_block, z_send.at[g, i - 1], z_recv.at[g, i - 1],
+            device_id=z_peers[i - 1], device_id_type=MESH,
+        )
+
+    def x_copy(g, i, way):
+        block = kv.at[g, :, block_rows(depths[i], x), :]
         return pltpu.make_async_remote_copy(
-            column(g, x), column(g, x), x_send.at[g, way], x_recv.at[g, way],
-            device_id=(right, left)[way], device_id_type=MESH,
-        )
-
-    def d_copy(g, way):
-        source = ((x + 3) % ALONG_X, (x + 1) % ALONG_X)[way]
-        return pltpu.make_async_remote_copy(
-            half_column(g, way, source), half_column(g, way, source),
-            d_send.at[g, way], d_recv.at[g, way],
-            device_id=(right, left)[way], device_id_type=MESH,
-        )
-
-    pl.semaphore_wait(barrier, 5)
-    for g in range(2):
-        for d in (1, 0, 2):
-            for kind in range(2):
-                z_copy(g, kind, d).start()
+            block, block, x_send.at[g, i, way], x_recv.at[g, i, way],
+            device_id=(right, left, across)[way], device_id_type=MESH,
+        )
+
+    def forward_x(g, i):
+        for way in range(3):
+            x_copy(g, i, way).start()
+
+    def gathered(g):
+        for i in range(ALONG_Z):
+            for way in range(3):
+                x_copy(g, i, way).wait_recv()
+
+    def top_two(keep, one, two, three):
+        first = jnp.where(keep == 1, one, jnp.where(keep == 2, two, three))
+        return first, jnp.where(keep == 1, two, three)
+
+    early_copies = [
+        pltpu.make_async_remote_copy(
+            e_send, e_recv, es_sem.at[0], er_sem.at[0],
+            device_id=first_partner, device_id_type=MESH,
+        ),
+        pltpu.make_async_remote_copy(
+            l_send, l_recv, es_sem.at[1], er_sem.at[1],
+            device_id=first_partner, device_id_type=MESH,
+        ),
+    ]
+
     for copy in own_copies:
         copy.wait()
-    for g in range(2):
-        for d in range(3):
-            for kind in range(2):
-                z_copy(g, kind, d).wait_recv()
-        for way in range(2):
-            x_copy(g, way).start()
+    pl.semaphore_wait(barrier, 6)
+    for i in (3, 1, 2):
+        z_copy(0, i).start()
+    forward_x(0, 0)
+
     for copy in in_copies:
         copy.wait()
-
-    def forward_diagonal(g):
-        for way in range(2):
-            x_copy(g, way).wait_recv()
-            d_copy(g, way).start()
-
-    def gathered(g):
-        for way in range(2):
-            d_copy(g, way).wait_recv()
-
-    forward_diagonal(0)
-
-    def s1_copy(c):
+    lane = lax.broadcasted_iota(jnp.int32, (TILE_TOKENS, width), 1)
+    levels = jnp.zeros((TILE_TOKENS, width), jnp.float32)
+    for e in range(EARLY):
+        c = EARLY_FROM + e
+        g = c // QUERY_PER_KEY
+        mixes, sums = [], []
+        for h in range(2):
+            rows = slice(2 * h * TILE_TOKENS, 2 * (h + 1) * TILE_TOKENS)
+            cols = slice(c * width, (c + 1) * width)
+            top, total, mix = reply_part(q_buf[rows, cols], rkv.at[g, 0], rkv.at[g, 1], h)
+            mix = (mix * (1.0 / total)).astype(jnp.bfloat16)
+            level = top * LOG_SCALE + jnp.log2(total)
+            mixes += [mix[:TILE_TOKENS], mix[TILE_TOKENS:]]
+            sums += [level[:TILE_TOKENS], level[TILE_TOKENS:]]
+        ask = [
+            q_buf[t * TILE_TOKENS : (t + 1) * TILE_TOKENS, c * width : (c + 1) * width]
+            for t in range(MOST_TILES)
+        ]
+        for kind, tiles in enumerate((ask, mixes)):
+            for j, tile in enumerate(top_two(keep1, *tiles[1:])):
+                e_send[e, kind, j * TILE_TOKENS : (j + 1) * TILE_TOKENS] = tile
+        for j, level in enumerate(top_two(keep1, *sums[1:])):
+            levels = jnp.where(lane == 2 * e + j, level, levels)
+    l_send[...] = levels.T[:8]
+
+    for copy in early_copies:
+        copy.start()
+    for i in (1, 2, 3):
+        z_copy(1, i).start()
+    for i in (1, 3, 2):
+        z_copy(0, i).wait_recv()
+        forward_x(0, i)
+
+    height = TILE_TOKENS // PARTS
+
+    def rows_of(part):
+        return slice(part * height, (part + 1) * height)
+
+    def s1_copy(c, part):
         return pltpu.make_async_remote_copy(
-            send1.at[c], recv1.at[c], s1_sem.at[c], r1_sem.at[c],
+            send1.at[c, :, rows_of(part), :], recv1.at[c, :, rows_of(part), :],
+            s1_sem.at[c, part], r1_sem.at[c, part],
             device_id=first_partner, device_id_type=MESH,
         )
 
-    def s2_copy(c):
+    def s2_copy(c, part):
         return pltpu.make_async_remote_copy(
-            send2.at[c], recv2.at[c], s2_sem.at[c], r2_sem.at[c],
+            send2.at[c, :, rows_of(part), :], recv2.at[c, :, rows_of(part), :],
+            s2_sem.at[c, part], r2_sem.at[c, part],
             device_id=second_partner, device_id_type=MESH,
         )
 
@@ -193,10 +240,6 @@
             out_hbm.at[:, :, pl.ds(pl.multiple_of(c * width, width), width)],
             out_sem.at[c],
         )
-
-    def top_two(keep, one, two, three):
-        first = jnp.where(keep == 1, one, jnp.where(keep == 2, two, three))
-        return first, jnp.where(keep == 1, two, three)
 
     def placed(keep, one, two, three, a, b):
         return (
@@ -236,32 +279,74 @@
         send1[c, 0] = first
         send1[c, 1] = second
 
+    def arrived(e):
+        c = EARLY_FROM + e
+        g = c // QUERY_PER_KEY
+        scores = dot_nt(e_recv[e, 0], kv[g, 0])
+        top, weights, total = softmax_parts(scores)
+        mix = weigh(weights, kv[g, 1])
+        spread = jnp.concatenate(
+            [l_recv[...], jnp.zeros((TILE_TOKENS - 8, width), jnp.float32)], axis=0
+        ).T
+        level = jnp.concatenate([spread[:, 2 * e : 2 * e + 1], spread[:, 2 * e + 1 : 2 * e + 2]], axis=0)
+        result = combine_level(top, total, mix, level, e_recv[e, 1])
+        recv1[c, 0] = result[:TILE_TOKENS]
+        recv1[c, 1] = result[TILE_TOKENS:]
+
     def step(c, _):
         @pl.when(c < HEADS)
         def _():
             attend(c)
-            s1_copy(c).start()
+
+        late = (c < EARLY_FROM) | (c >= EARLY_FROM + EARLY)
+
+        @pl.when((c < HEADS) & late)
+        def _():
+            for part in range(PARTS):
+                s1_copy(c, part).start()
+
+        @pl.when(c == EARLY_FROM)
+        def _():
+            for copy in early_copies:
+                copy.wait_recv()
+
+        for e in range(EARLY):
+            @pl.when(c == EARLY_FROM + e)
+            def _():
+                arrived(e)
 
         @pl.when(c == 0)
         def _():
-            forward_diagonal(1)
+            for i in (1, 2, 3):
+                z_copy(1, i).wait_recv()
+            for i in range(ALONG_Z):
+                forward_x(1, i)
 
         @pl.when((c >= LAG_SECOND) & (c < HEADS + LAG_SECOND))
         def _():
             d = c - LAG_SECOND
-            s1_copy(d).wait_recv()
-            slots = placed(keep1, own[d, 1], own[d, 2], own[d, 3], recv1[d, 0], recv1[d, 1])
-            first, second = top_two(keep2, *slots)
-            send2[d, 0] = first
-            send2[d, 1] = second
-            s2_copy(d).start()
-            for t in range(3):
-                own[d, t + 1] = slots[t]
+            waits = (d < EARLY_FROM) | (d >= EARLY_FROM + EARLY)
+            for part in range(PARTS):
+                r = rows_of(part)
+
+                @pl.when(waits)
+                def _():
+                    s1_copy(d, part).wait_recv()
+
+                mine = [own[d, t, r] for t in (1, 2, 3)]
+                slots = placed(keep1, *mine, recv1[d, 0, r], recv1[d, 1, r])
+                first, second = top_two(keep2, *slots)
+                send2[d, 0, r] = first
+                send2[d, 1, r] = second
+                s2_copy(d, part).start()
+                for t in range(3):
+                    own[d, t + 1, r] = slots[t]
 
         @pl.when(c >= LAG_OUT)
         def _():
             e = c - LAG_OUT
-            s2_copy(e).wait_recv()
+            for part in range(PARTS):
+                s2_copy(e, part).wait_recv()
             slots = placed(keep2, own[e, 1], own[e, 2], own[e, 3], recv2[e, 0], recv2[e, 1])
             out_buf[e, 0] = own[e, 0]
             for t in range(3):
@@ -273,16 +358,23 @@
     lax.fori_loop(0, HEADS + LAG_OUT, step, 0)
 
     for g in range(2):
-        for d in range(3):
-            for kind in range(2):
-                z_copy(g, kind, d).wait_send()
-        for way in range(2):
-            x_copy(g, way).wait_send()
-            d_copy(g, way).wait_send()
+        for i in (1, 2, 3):
+            z_copy(g, i).wait_send()
+        for i in range(ALONG_Z):
+            for way in range(3):
+                x_copy(g, i, way).wait_send()
+
+    for copy in early_copies:
+        copy.wait_send()
 
     def finish(c, _):
-        s1_copy(c).wait_send()
-        s2_copy(c).wait_send()
+        @pl.when((c < EARLY_FROM) | (c >= EARLY_FROM + EARLY))
+        def _():
+            for part in range(PARTS):
+                s1_copy(c, part).wait_send()
+
+        for part in range(PARTS):
+            s2_copy(c, part).wait_send()
         out_copy(c).wait()
         return 0
 
@@ -300,7 +392,7 @@
     scalars = pl.BlockSpec(memory_space=pltpu.SMEM)
     out = pl.pallas_call(
         kernel,
-        out_shape=jax.ShapeDtypeStruct((MOST_TILES, TILE_TOKENS, HEADS * HEAD_WIDTH), half),
+        out_shape=pltpu.VMEM((MOST_TILES, TILE_TOKENS, HEADS * HEAD_WIDTH), half),
         in_specs=[anywhere] * 5 + [scalars] * 2,
         out_specs=anywhere,
         scratch_shapes=[
@@ -313,19 +405,23 @@
             pltpu.VMEM(pair, half),
             pltpu.VMEM(pair, half),
             pltpu.VMEM(four, half),
+            pltpu.VMEM((EARLY, 2, 2 * TILE_TOKENS, HEAD_WIDTH), half),
+            pltpu.VMEM((EARLY, 2, 2 * TILE_TOKENS, HEAD_WIDTH), half),
+            pltpu.VMEM((8, HEAD_WIDTH), jnp.float32),
+            pltpu.VMEM((8, HEAD_WIDTH), jnp.float32),
             dma((5,)),
             dma((2, 2)),
-            dma((2, 2, 3)),
-            dma((2, 2, 3)),
-            dma((2, 2)),
-            dma((2, 2)),
-            dma((2, 2)),
-            dma((2, 2)),
+            dma((2, 3)),
+            dma((2, 3)),
+            dma((2, ALONG_Z, 3)),
+            dma((2, ALONG_Z, 3)),
+            dma((HEADS, PARTS)),
+            dma((HEADS, PARTS)),
+            dma((HEADS, PARTS)),
+            dma((HEADS, PARTS)),
             dma((HEADS,)),
-            dma((HEADS,)),
-            dma((HEADS,)),
-            dma((HEADS,)),
-            dma((HEADS,)),
+            dma((2,)),
+            dma((2,)),
         ],
         compiler_params=pltpu.CompilerParams(
             collective_id=0, has_side_effects=True, vmem_limit_bytes=56 << 20

time: 72.5 us -> 65.2 us (0.90)
  Pallas kernels: 69.5 us -> 63.8 us
  local copies, waits for them, and re-layouts: 2.85 us -> 1.23 us
    pallas_call x1, Pallas kernels: 69.5 us -> 63.8 us  [per_device(): pl.pallas_call(kernel, out_shape=pltpu.VMEM((MOST_TILES, TILE_TOKENS, HEA...]
    unnamed x1, local copies, waits for them, and re-layouts: 2.85 us -> 1.23 us
where the time goes in v1:
time: 65.2 us; the launch traced here: 65 us
  Pallas kernels  63.8 us (98%)
  local copies, waits for them, and re-layouts  1.23 us (2%)
    pallas_call x1, Pallas kernels, per_device(): pl.pallas_call(kernel, out_shape=pltpu.VMEM((MOST_TILES, TILE_TOKENS, HEA...  63.8 us

profile of v1, /device:TPU:136, one launch (start us, length us, event | category | flops | bytes accessed | tf_op | source)
XLA Modules:
  0.0 65.0 jit_solution(5059970029310349289)
XLA Ops:
  0.0 63.8 %shard_map.73 = bf16[4,128,1792]{2,1,0:T(8,128)(2,1)S(1)} custom-call(bf16[512,1792]{1,0:T(8,128)(2,1)} %bitcast.8, bf16[64,256]{1,0:T(8,128)(2,1)} %bitcast.11, bf16[64,256]{1,0:T(8,128)(2,1)} %bitcast.12, bf16[512,256]{1,0:T(8,128)(2,1)} %bitcast.9, bf16[512,256]{1,0:T(8,128)(2,1)} %bitcast.10, s32[1,16]{1,0:T(1,128)} %len_ref.1, s32[1,2,16]{2,1,0:T(2,128)} %bitcast.13), custom_call_target="tpu_custom_call" | custom-call | tf_op jit(solution)/shard_map/pallas_call | solution.py:393
  63.8 1.2 %copy.9 = bf16[1,512,1792]{2,1,0:T(8,128)(2,1)} copy(bf16[1,512,1792]{2,1,0:T(8,128)(2,1)S(1)} %bitcast.7) | data formatting | bytes 3670016

commit v2 on v1

--- a/solution.py
+++ b/solution.py
@@ -62,12 +62,28 @@
     return (p_mix * (a * inverse) + r_mix.astype(jnp.float32) * (b * inverse)).astype(jnp.bfloat16)
 
 
-def combine(p_top, p_total, p_mix, r_top, r_total, r_mix):
-    top = jnp.maximum(p_top, r_top)
-    a = jnp.exp2((p_top - top) * LOG_SCALE)
-    b = jnp.exp2((r_top - top) * LOG_SCALE)
-    inverse = 1.0 / (a * p_total + b * r_total)
-    return (p_mix * (a * inverse) + r_mix * (b * inverse)).astype(jnp.bfloat16)
+def joint_part(query, p_keys, p_values, r_keys, r_values, half):
+    rows = 2 * TILE_TOKENS
+    seen = (half + 1) * rows
+    scores = dot_nt(query, r_keys[:seen])
+    row = lax.broadcasted_iota(jnp.int32, (rows, rows), 0)
+    col = lax.broadcasted_iota(jnp.int32, (rows, rows), 1)
+    pieces = [jnp.where(col <= row, scores[:, half * rows :], -1e30)]
+    values = [r_values[half * rows : seen]]
+    if half:
+        pieces.append(scores[:, :rows])
+        values.append(r_values[:rows])
+    pieces.append(dot_nt(query, p_keys))
+    values.append(p_values)
+    top = functools.reduce(
+        jnp.maximum, [jnp.max(piece, axis=-1, keepdims=True) for piece in pieces]
+    )
+    total, mix = 0.0, 0.0
+    for piece, value in zip(pieces, values):
+        weights = jnp.exp2((piece - top) * LOG_SCALE)
+        total = total + jnp.sum(weights, axis=-1, keepdims=True)
+        mix = mix + weigh(weights.astype(jnp.bfloat16), value)
+    return (mix * (1.0 / total)).astype(jnp.bfloat16)
 
 
 def kernel(
@@ -136,10 +152,10 @@
         return pl.ds(pl.multiple_of(xx * 256 + zz * 64, 64), 64)
 
     def z_copy(g, i):
-        own_block = kv.at[g, :, own_rows, :]
+        block = kv.at[g, :, block_rows(depths[2 if i == 3 else 0], x), :]
         return pltpu.make_async_remote_copy(
-            own_block, own_block, z_send.at[g, i - 1], z_recv.at[g, i - 1],
-            device_id=z_peers[i - 1], device_id_type=MESH,
+            block, block, z_send.at[g, i - 1], z_recv.at[g, i - 1],
+            device_id=z_peers[0 if i == 3 else i - 1], device_id_type=MESH,
         )
 
     def x_copy(g, i, way):
@@ -150,7 +166,7 @@
         )
 
     def forward_x(g, i):
-        for way in range(3):
+        for way in (2, 0, 1):
             x_copy(g, i, way).start()
 
     def gathered(g):
@@ -176,7 +192,7 @@
     for copy in own_copies:
         copy.wait()
     pl.semaphore_wait(barrier, 6)
-    for i in (3, 1, 2):
+    for i in (2, 1):
         z_copy(0, i).start()
     forward_x(0, 0)
 
@@ -207,13 +223,17 @@
             levels = jnp.where(lane == 2 * e + j, level, levels)
     l_send[...] = levels.T[:8]
 
+    z_copy(0, 1).wait_recv()
+    forward_x(0, 1)
+    z_copy(0, 2).wait_recv()
+    z_copy(0, 3).start()
+    forward_x(0, 2)
     for copy in early_copies:
         copy.start()
-    for i in (1, 2, 3):
+    for i in (2, 1):
         z_copy(1, i).start()
-    for i in (1, 3, 2):
-        z_copy(0, i).wait_recv()
-        forward_x(0, i)
+    z_copy(0, 3).wait_recv()
+    forward_x(0, 3)
 
     height = TILE_TOKENS // PARTS
 
@@ -252,26 +272,12 @@
         g = c // QUERY_PER_KEY
         cols = pl.ds(pl.multiple_of(c * width, width), width)
         rows = 2 * TILE_TOKENS
-        reply = [
-            reply_part(q_buf[h * rows : (h + 1) * rows, cols], rkv.at[g, 0], rkv.at[g, 1], h)
-            for h in range(2)
-        ]
-
-        @pl.when(c == 0)
-        def _():
-            gathered(0)
-
-        @pl.when(c == QUERY_PER_KEY)
-        def _():
-            gathered(1)
-
         tiles = []
         for h in range(2):
-            scores = dot_nt(q_buf[h * rows : (h + 1) * rows, cols], kv[g, 0])
-            top, weights, total = softmax_parts(scores)
-            mix = weigh(weights, kv[g, 1])
-            r_top, r_total, r_mix = reply[h]
-            result = combine(top, total, mix, r_top, r_total, r_mix)
+            result = joint_part(
+                q_buf[h * rows : (h + 1) * rows, cols],
+                kv[g, 0], kv[g, 1], rkv.at[g, 0], rkv.at[g, 1], h,
+            )
             tiles += [result[:TILE_TOKENS], result[TILE_TOKENS:]]
         for t in range(MOST_TILES):
             own[c, t] = tiles[t]
@@ -294,6 +300,14 @@
         recv1[c, 1] = result[TILE_TOKENS:]
 
     def step(c, _):
+        @pl.when(c == 0)
+        def _():
+            gathered(0)
+
+        @pl.when(c == QUERY_PER_KEY)
+        def _():
+            gathered(1)
+
         @pl.when(c < HEADS)
         def _():
             attend(c)
@@ -317,10 +331,16 @@
 
         @pl.when(c == 0)
         def _():
-            for i in (1, 2, 3):
+            for i in (1, 2):
                 z_copy(1, i).wait_recv()
-            for i in range(ALONG_Z):
+            z_copy(1, 3).start()
+            for i in range(3):
                 forward_x(1, i)
+
+        @pl.when(c == 2)
+        def _():
+            z_copy(1, 3).wait_recv()
+            forward_x(1, 3)
 
         @pl.when((c >= LAG_SECOND) & (c < HEADS + LAG_SECOND))
         def _():

time: 65.2 us -> 64.1 us (0.983)
  the two profiles are of different devices: /device:TPU:136 before, /device:TPU:6 now
where the time goes in v2:
time: 64.1 us; the launch traced here: 63.9 us
  Pallas kernels  62.7 us (98%)
  local copies, waits for them, and re-layouts  1.23 us (2%)
    pallas_call x1, Pallas kernels, per_device(): pl.pallas_call(kernel, out_shape=pltpu.VMEM((MOST_TILES, TILE_TOKENS, HEA...  62.7 us

profile of v2, /device:TPU:6, one launch (start us, length us, event | category | flops | bytes accessed | tf_op | source)
XLA Modules:
  0.0 63.9 jit_solution(125984385883394106)
XLA Ops:
  0.0 62.7 %shard_map.73 = bf16[4,128,1792]{2,1,0:T(8,128)(2,1)S(1)} custom-call(bf16[512,1792]{1,0:T(8,128)(2,1)} %bitcast.8, bf16[64,256]{1,0:T(8,128)(2,1)} %bitcast.11, bf16[64,256]{1,0:T(8,128)(2,1)} %bitcast.12, bf16[512,256]{1,0:T(8,128)(2,1)} %bitcast.9, bf16[512,256]{1,0:T(8,128)(2,1)} %bitcast.10, s32[1,16]{1,0:T(1,128)} %len_ref.1, s32[1,2,16]{2,1,0:T(2,128)} %bitcast.13), custom_call_target="tpu_custom_call" | custom-call | tf_op jit(solution)/shard_map/pallas_call | solution.py:413
  62.7 1.2 %copy.9 = bf16[1,512,1792]{2,1,0:T(8,128)(2,1)} copy(bf16[1,512,1792]{2,1,0:T(8,128)(2,1)S(1)} %bitcast.7) | data formatting | bytes 3670016
